TPU v7x, 256 devices: a whole 4x4x8 slice. The times are simulated.
256 devices in a mesh: row: 16 (over z, core), col: 8 (over x_hi, y), lrn: 2 (over x_lo).
Axes of the slice: x: 4 (x_hi: 2, x_lo: 2; x = x_hi * 2 + x_lo), y: 4, z: 8, core: 2. Of those that a mesh axis runs over, the one named last changes fastest.
Arguments:
- responses: int32 [4096, 16384], P('lrn', ('row', 'col')), may hold values 0 or 1
- observed: int32 [4096, 16384], P('lrn', ('row', 'col')), may hold values from 0 to 1, as said below
- qmatrix: int32 [16384, 8], P(('row', 'col')), may hold values from 0 to 1
- guess: float32 [16384], P(('row', 'col')), may hold values from 0.05 to 0.35
- slip: float32 [16384], P(('row', 'col')), may hold values from 0.05 to 0.35
Outputs:
- q3_scaled: float32 [16384, 16384], P('row', ('col', 'lrn'))
Inputs may be any that keep to these rules, and one draw needn't show every extreme that they name: Some items have no observed response from any learner.
All inputs are finite; a program needn't handle non-finite values. No bound on the sum of `responses` on one device may be relied on, other than what follows from the above.
Results may differ from a plain program's by a relative error of at most 0.008.
Values may be sent and summed in bfloat16 or wider, within the bound.
No kernel may reach another device: no remote copies, remote signals or barrier semaphores. Data moves between devices by JAX's collectives and lax.ppermute only.
A program may use at most 128 MiB of HBM per device.

v0:
```python
import jax
import jax.numpy as jnp
from jax import lax
from jax.sharding import PartitionSpec as P

ATTRS = 8
PROFILES = 256


def spread(x, axis, root):
    mine = lax.axis_index(axis) == root
    return lax.psum(jnp.where(mine, x, jnp.zeros_like(x)), axis)


def success(qmatrix, guess, slip):
    codes = jnp.arange(PROFILES, dtype=jnp.int32)
    powers = jnp.arange(ATTRS, dtype=jnp.int32)
    bits = (codes[None, :] >> powers[:, None] & 1).astype(jnp.float32)
    lacking = jnp.dot(qmatrix.astype(jnp.float32), 1.0 - bits, precision=lax.Precision.HIGHEST)
    return jnp.where(lacking == 0.0, 1.0 - slip[:, None], guess[:, None])


def learner_product(left, right):
    return lax.dot_general(
        left, right, (((0,), (0,)), ((), ())), preferred_element_type=jnp.float32
    )


def shards(responses, observed, qmatrix, guess, slip):
    prob = success(qmatrix, guess, slip)
    answered = responses.astype(jnp.float32)
    seen = observed.astype(jnp.float32)
    partial_value = jnp.dot(seen * answered, jnp.log(prob), precision=lax.Precision.HIGHEST)
    partial_value = partial_value + jnp.dot(
        seen * (1.0 - answered), jnp.log(1.0 - prob), precision=lax.Precision.HIGHEST
    )
    loglik = lax.psum(partial_value, ("row", "col"))
    posterior = jax.nn.softmax(loglik, axis=1).astype(jnp.bfloat16)
    expected = jnp.dot(posterior, prob.astype(jnp.bfloat16).T, preferred_element_type=jnp.float32)
    resid = seen * (answered - expected)
    count, total, square = lax.psum(
        (jnp.sum(seen, axis=0), jnp.sum(resid, axis=0), jnp.sum(resid * resid, axis=0)), "lrn"
    )
    count = jnp.maximum(count, 1.0)
    mean = total / count
    var = square / count - mean * mean
    zres = (seen * (resid - mean) * lax.rsqrt(var + 1e-06) * lax.rsqrt(count)).astype(jnp.bfloat16)
    panel = lax.all_gather(zres, "col", axis=1, tiled=True)
    learner_total = zres.shape[0] * lax.axis_size("lrn")
    whole_panel = lax.all_gather(panel, "lrn", axis=0, tiled=True)
    repeats = lax.axis_size("row") // (lax.axis_size("col") * lax.axis_size("lrn"))
    tile_index = lax.axis_index("col") * lax.axis_size("lrn") + lax.axis_index("lrn")
    pieces = spread(whole_panel, "row", tile_index * repeats + 0)
    gram = learner_product(whole_panel, pieces)
    return gram * jnp.sqrt(jnp.float32(learner_total))


def solution(mesh):
    placed = (
        P("lrn", ("row", "col")),
        P("lrn", ("row", "col")),
        P(("row", "col"), None),
        P(("row", "col")),
        P(("row", "col")),
    )
    return jax.shard_map(
        shards, mesh=mesh, in_specs=placed, out_specs=P("row", ("col", "lrn")), check_vma=False
    )
```

profile of v0, /device:TPU:2, one launch (start us, length us, event | category | flops | bytes accessed | tf_op | source)
XLA Modules:
  0.0 1652.2 jit_solution(6100974589586948307)
XLA Ops:
  6.5 0.0 copy-start
  6.5 0.0 copy-start.1
  6.5 0.0 all-reduce.4.cloned.1.call-start
  6.5 0.8 broadcast_subtract_fusion
  7.3 1.1 fusion
  8.4 0.0 copy-start.2
  8.5 3.4 fusion.3
  11.9 0.0 copy-done
  11.9 0.0 copy-done.1
  11.9 3.2 convolution_add_fusion
  15.1 0.0 copy-done.2
  15.1 0.0 all-reduce.4.cloned.1.call-update
  15.1 0.0 all-gather.3.cloned.1.call-start
  15.1 1279.9 %all-reduce.4.cloned.1.call-done = f32[2048,256]{1,0:T(8,128)} async-done(((f32[2048,256]{1,0:T(8,128)}), f32[2048,256]{1,0:T(8,128)}) %all-reduce.4.cloned.1.call-update) | async-done | bytes 2097168 | tf_op jit(solution)/shard_map/psum | solution.py:37
  1295.0 3.9 online-softmax
  1298.9 1.5 multiply_reduce_fusion
  1300.4 4.9 all-reduce
  1305.4 1.0 multiply_convert_fusion
  1306.4 0.0 all-gather.3.cloned.1.call-update
  1306.4 0.0 all-gather.5.cloned.1.call-start
  1306.5 72.4 %all-gather.3.cloned.1.call-done = bf16[2048,1024]{1,0:T(8,128)(2,1)} async-done(((bf16[2048,128]{1,0:T(8,128)(2,1)}), bf16[2048,1024]{1,0:T(8,128)(2,1)}) %all-gather.3.cloned.1.call-update) | async-done | bytes 4194320 | tf_op jit(solution)/shard_map/all_gather | solution.py:48
  1378.8 0.0 all-gather.5.cloned.1.call-update
  1378.9 0.0 all-reduce.6.cloned.1.call-start
  1378.9 108.7 %all-gather.5.cloned.1.call-done = bf16[4096,1024]{1,0:T(8,128)(2,1)} async-done(((bf16[2048,1024]{1,0:T(8,128)(2,1)}), bf16[4096,1024]{1,0:T(8,128)(2,1)}) %all-gather.5.cloned.1.call-update) | async-done | bytes 8388624 | tf_op jit(solution)/shard_map/all_gather | solution.py:50
  1487.6 3.8 broadcast_select_fusion
  1491.4 0.0 all-reduce.6.cloned.1.call-update
  1491.4 139.2 %all-reduce.6.cloned.1.call-done = bf16[4096,1024]{1,0:T(8,128)(2,1)} async-done(((bf16[4096,1024]{1,0:T(8,128)(2,1)}), bf16[4096,1024]{1,0:T(8,128)(2,1)}) %all-reduce.6.cloned.1.call-update) | async-done | bytes 8388624 | tf_op jit(solution)/shard_map/psum | solution.py:12
  1630.6 15.0 convolution_multiply_fusion
  (1 shorter events, 0.0 us)
Async XLA Ops:
  6.5 5.4 copy-start
  6.5 5.4 copy-start.1
  6.5 1288.5 %all-reduce.4.cloned.1.call-start = ((), (), s32[]{:S(2)}) async-start(), calls=%async_computation | async-start | bytes 4194304 | tf_op jit(solution)/shard_map/psum | solution.py:37
  8.4 6.6 copy-start.2
  15.1 1363.7 %all-gather.3.cloned.1.call-start = ((), (), s32[]{:S(2)}) async-start(), calls=%async_computation.1 | async-start | bytes 4718592 | tf_op jit(solution)/shard_map/all_gather | solution.py:48
  1306.4 181.2 %all-gather.5.cloned.1.call-start = ((), (), s32[]{:S(2)}) async-start(), calls=%async_computation.2 | async-start | bytes 12582912 | tf_op jit(solution)/shard_map/all_gather | solution.py:50
  1378.9 251.8 %all-reduce.6.cloned.1.call-start = ((), (), s32[]{:S(2)}) async-start(), calls=%async_computation.3 | async-start | bytes 16777216 | tf_op jit(solution)/shard_map/psum | solution.py:12
Sparse Core Ops, SparseCore 0:
  15.2 1279.7 all-reduce.3
  1306.5 72.2 all-gather.2
  1380.8 106.7 all-gather.4
  1491.5 139.0 all-reduce.5
where the time goes:
time: 1650 us
  waiting for transfers between devices  1600 us (97%)
  matrix products  22.7 us (1%)
    psum x1, waiting for transfers between devices, shards(): loglik = lax.psum(partial_value, ('row', 'col'))  1280 us
    psum x1, waiting for transfers between devices, spread(): return lax.psum(jnp.where(mine, x, jnp.zeros_like(x)), axis)  139 us
    all_gather x1, waiting for transfers between devices, shards(): whole_panel = lax.all_gather(panel, 'lrn', axis=0, tiled=True)  109 us
    all_gather x1, waiting for transfers between devices, shards(): panel = lax.all_gather(zres, 'col', axis=1, tiled=True)  72.4 us
  transfers between devices with their start and end apart: 4, of which 4 were waited for; matrix products, arithmetic and copies ran while one was open for 0% of the time, Pallas kernels for 0%

commit v1 on v0

--- a/solution.py
+++ b/solution.py
@@ -34,7 +34,8 @@
     partial_value = partial_value + jnp.dot(
         seen * (1.0 - answered), jnp.log(1.0 - prob), precision=lax.Precision.HIGHEST
     )
-    loglik = lax.psum(partial_value, ("row", "col"))
+    partial = lax.psum(partial_value, "row")
+    loglik = lax.psum(partial, "col")
     posterior = jax.nn.softmax(loglik, axis=1).astype(jnp.bfloat16)
     expected = jnp.dot(posterior, prob.astype(jnp.bfloat16).T, preferred_element_type=jnp.float32)
     resid = seen * (answered - expected)

time: 1650 us -> 595 us (0.36)
  waiting for transfers between devices: 1600 us -> 543 us
    psum x1 -> x2, waiting for transfers between devices: 1280 us -> 217 us  [the longest x1 118 us: shards(): partial = lax.psum(partial_value, 'row')]
  transfers between devices with their start and end apart: 4 -> 5, of which waited for: 4 -> 5; matrix products, arithmetic and copies ran while one was open for 0% -> 0% of each run, Pallas kernels for 0% -> 0%
where the time goes in v1:
time: 595 us
  waiting for transfers between devices  543 us (91%)
  matrix products  22.7 us (4%)
  between operations  13.2 us (2%)
  other arithmetic  7.1 us (1%)
    psum x1, waiting for transfers between devices, spread(): return lax.psum(jnp.where(mine, x, jnp.zeros_like(x)), axis)  139 us
    psum x1, waiting for transfers between devices, shards(): partial = lax.psum(partial_value, 'row')  118 us
    all_gather x1, waiting for transfers between devices, shards(): whole_panel = lax.all_gather(panel, 'lrn', axis=0, tiled=True)  108 us
    psum x1, waiting for transfers between devices, shards(): loglik = lax.psum(partial, 'col')  99.4 us
    all_gather x1, waiting for transfers between devices, shards(): panel = lax.all_gather(zres, 'col', axis=1, tiled=True)  77.5 us
    dot_general x1, matrix products, learner_product(): lax.dot_general(left, right, (((0,), (0,)), ((), ())), preferred_element_...  15 us
  transfers between devices with their start and end apart: 5, of which 5 were waited for; matrix products, arithmetic and copies ran while one was open for 0% of the time, Pallas kernels for 0%

profile of v1, /device:TPU:2, one launch (start us, length us, event | category | flops | bytes accessed | tf_op | source)
XLA Modules:
  0.0 594.7 jit_solution(11264202702036551961)
XLA Ops:
  6.5 0.0 copy-start
  6.5 0.0 copy-start.1
  6.5 0.0 all-reduce.5.cloned.1.call-start
  6.5 0.8 broadcast_subtract_fusion
  7.3 1.1 fusion
  8.4 0.0 copy-start.2
  8.5 3.4 fusion.3
  11.9 0.0 copy-done
  11.9 0.0 copy-done.1
  11.9 3.2 convolution_add_fusion
  15.1 0.0 copy-done.2
  15.1 0.0 all-reduce.5.cloned.1.call-update
  15.1 0.0 all-reduce.7.cloned.1.call-start
  15.1 118.0 %all-reduce.5.cloned.1.call-done = f32[2048,256]{1,0:T(8,128)} async-done(((f32[2048,256]{1,0:T(8,128)}), f32[2048,256]{1,0:T(8,128)}) %all-reduce.5.cloned.1.call-update) | async-done | bytes 2097168 | tf_op jit(solution)/shard_map/psum | solution.py:37
  133.2 0.0 all-reduce.7.cloned.1.call-update
  133.2 0.0 all-gather.3.cloned.1.call-start
  133.3 99.4 %all-reduce.7.cloned.1.call-done = f32[2048,256]{1,0:T(8,128)} async-done(((f32[2048,256]{1,0:T(8,128)}), f32[2048,256]{1,0:T(8,128)}) %all-reduce.7.cloned.1.call-update) | async-done | bytes 2097168 | tf_op jit(solution)/shard_map/psum | solution.py:38
  232.6 3.9 online-softmax
  236.5 1.5 multiply_reduce_fusion
  238.1 4.9 all-reduce
  243.0 1.0 multiply_convert_fusion
  244.0 0.0 all-gather.3.cloned.1.call-update
  244.1 0.0 all-gather.5.cloned.1.call-start
  244.1 77.5 %all-gather.3.cloned.1.call-done = bf16[2048,1024]{1,0:T(8,128)(2,1)} async-done(((bf16[2048,128]{1,0:T(8,128)(2,1)}), bf16[2048,1024]{1,0:T(8,128)(2,1)}) %all-gather.3.cloned.1.call-update) | async-done | bytes 4194320 | tf_op jit(solution)/shard_map/all_gather | solution.py:49
  321.6 0.0 all-gather.5.cloned.1.call-update
  321.6 0.0 all-reduce.9.cloned.1.call-start
  321.7 108.4 %all-gather.5.cloned.1.call-done = bf16[4096,1024]{1,0:T(8,128)(2,1)} async-done(((bf16[2048,1024]{1,0:T(8,128)(2,1)}), bf16[4096,1024]{1,0:T(8,128)(2,1)}) %all-gather.5.cloned.1.call-update) | async-done | bytes 8388624 | tf_op jit(solution)/shard_map/all_gather | solution.py:51
  430.1 3.8 broadcast_select_fusion
  433.8 0.0 all-reduce.9.cloned.1.call-update
  433.9 139.2 %all-reduce.9.cloned.1.call-done = bf16[4096,1024]{1,0:T(8,128)(2,1)} async-done(((bf16[4096,1024]{1,0:T(8,128)(2,1)}), bf16[4096,1024]{1,0:T(8,128)(2,1)}) %all-reduce.9.cloned.1.call-update) | async-done | bytes 8388624 | tf_op jit(solution)/shard_map/psum | solution.py:12
  573.1 15.0 %convolution_multiply_fusion = f32[1024,1024]{1,0:T(8,128)} fusion(bf16[4096,1024]{1,0:T(8,128)(2,1)} %all-gather.5.cloned.1.call-done, bf16[4096,1024]{1,0:T(8,128)(2,1)} %all-reduce.9.cloned.1.call-done), kind=kOutput, calls=%fused_computation.2 | convolution fusion | flops 8590983168 | bytes 20971520 | tf_op jit(solution)/shard_map/dot_general | solution.py:24
  (1 shorter events, 0.0 us)
Async XLA Ops:
  6.5 5.4 copy-start
  6.5 5.4 copy-start.1
  6.5 126.6 %all-reduce.5.cloned.1.call-start = ((), (), s32[]{:S(2)}) async-start(), calls=%async_computation | async-start | bytes 4194304 | tf_op jit(solution)/shard_map/psum | solution.py:37
  8.4 6.6 %copy-start.2 = (f32[256,128]{1,0:T(8,128)}, f32[256,128]{1,0:T(8,128)S(1)}, u32[]{:S(2)}) copy-start(f32[256,128]{1,0:T(8,128)S(1)} %fusion) | copy-start | bytes 393220
  15.1 217.6 %all-reduce.7.cloned.1.call-start = ((), (), s32[]{:S(2)}) async-start(), calls=%async_computation.1 | async-start | bytes 4194304 | tf_op jit(solution)/shard_map/psum | solution.py:38
  133.2 188.4 %all-gather.3.cloned.1.call-start = ((), (), s32[]{:S(2)}) async-start(), calls=%async_computation.2 | async-start | bytes 4718592 | tf_op jit(solution)/shard_map/all_gather | solution.py:49
  244.1 186.0 %all-gather.5.cloned.1.call-start = ((), (), s32[]{:S(2)}) async-start(), calls=%async_computation.3 | async-start | bytes 12582912 | tf_op jit(solution)/shard_map/all_gather | solution.py:51
  321.6 251.5 %all-reduce.9.cloned.1.call-start = ((), (), s32[]{:S(2)}) async-start(), calls=%async_computation.4 | async-start | bytes 16777216 | tf_op jit(solution)/shard_map/psum | solution.py:12
Sparse Core Ops, SparseCore 0:
  15.2 117.9 all-reduce.4
  135.8 96.7 all-reduce.6
  244.2 77.3 all-gather.2
  323.2 106.7 all-gather.4
  434.0 139.0 all-reduce.8
